TPU v7x, 32 devices: a whole 2x2x4 slice. The times are simulated.
32 devices in a mesh: grp: 4 (over z), col: 8 (over y, x, core).
Axes of the slice: x: 2, y: 2, z: 4, core: 2. Of those that a mesh axis runs over, the one named last changes fastest.
Arguments:
- inverse: bfloat16 [4, 8192, 8192], P('grp', None, 'col'), as said below
- right_side: float32 [4, 8192, 256], P('grp', 'col'), may hold values from -6 to 6
- penalty: float32 [256], replicated, may hold values from 0.2 to 6
Outputs:
- consensus: float32 [8192, 256], P('col')
- duals: float32 [4, 8192, 256], P('grp', 'col')
Inputs may be any that keep to these rules, and one draw needn't show every extreme that they name: Each inverse[g] is symmetric.
All inputs are finite; a program needn't handle non-finite values.
Results may differ from a plain program's by a relative error of at most 0.0042.
Values may be sent and summed in bfloat16 or wider, within the bound.
A program may use at most 64 MiB of HBM per device.

v0:
```python
import jax
import jax.numpy as jnp
from jax import lax
from jax.sharding import PartitionSpec as P

ITERS = 3


def soft_shrink(values, limit):
    return jnp.sign(values) * jnp.maximum(jnp.abs(values) - limit, 0.0)


def apply_inverse(columns, shifted):
    return lax.dot_general(
        columns,
        lax.all_gather(shifted, "col", axis=0, tiled=True),
        (((0,), (0,)), ((), ())),
        preferred_element_type=jnp.float32,
    )


def agree(summed_in, limit, groups):
    summed = lax.psum(summed_in, "grp")
    return soft_shrink(summed / groups, limit[None, :])


def update_paths(columns, right_part, consensus, duals, limit, groups):
    shifted = (right_part + consensus - duals).astype(jnp.bfloat16)
    primal = apply_inverse(columns, shifted)
    consensus = agree(primal + duals, limit, groups)
    duals = duals + primal - consensus
    return (consensus, duals)


def on_device(inverse, right_side, penalty):
    columns = inverse[0]
    right_part = right_side[0]
    groups = lax.axis_size("grp")
    limit = penalty / groups
    consensus = jnp.zeros(right_part.shape, jnp.float32)
    duals = jnp.zeros(right_part.shape, jnp.float32)
    for step in range(ITERS):
        consensus, duals = update_paths(columns, right_part, consensus, duals, limit, groups)
    return (consensus, duals[None])


def solution(mesh):
    in_specs = (P("grp", None, "col"), P("grp", "col", None), P())
    out_specs = (P("col", None), P("grp", "col", None))
    return jax.shard_map(
        on_device, mesh=mesh, in_specs=in_specs, out_specs=out_specs, check_vma=False
    )
```

profile of v0, /device:TPU:0, one launch (start us, length us, event | category | flops | bytes accessed | tf_op | source)
XLA Modules:
  0.0 336.2 jit_solution(9609266918678891389)
XLA Ops:
  7.2 0.0 all-gather.4.cloned.1.call-start
  7.2 2.1 bitcast_convert_fusion
  9.3 0.0 all-gather.4.cloned.1.call-update
  9.3 0.0 all-reduce.4.cloned.1.call-start
  9.4 40.4 %all-gather.4.cloned.1.call-done = bf16[8192,256]{1,0:T(8,128)(2,1)} async-done(((bf16[1024,256]{1,0:T(8,128)(2,1)}), bf16[8192,256]{1,0:T(8,128)(2,1)}) %all-gather.4.cloned.1.call-update) | async-done | bytes 4194320 | tf_op jit(solution)/shard_map/all_gather | solution.py:16
  49.8 12.4 %fusion.4 = f32[1024,256]{1,0:T(8,128)} fusion(bf16[8192,256]{1,0:T(8,128)(2,1)} %all-gather.4.cloned.1.call-done, bf16[1,8192,1024]{2,1,0:T(8,128)(2,1)} %param.3), kind=kOutput, calls=%fused_computation.4 | convolution fusion | flops 4294967296 | bytes 22020096 | tf_op jit(solution)/shard_map/dot_general | solution.py:14
  62.2 0.0 all-reduce.4.cloned.1.call-update
  62.2 0.0 all-gather.6.cloned.1.call-start
  62.3 52.0 %all-reduce.4.cloned.1.call-done = f32[1024,256]{1,0:T(8,128)} async-done(((f32[1024,256]{1,0:T(8,128)}), f32[1024,256]{1,0:T(8,128)}) %all-reduce.4.cloned.1.call-update) | async-done | bytes 1048592 | tf_op jit(solution)/shard_map/psum | solution.py:23
  114.3 3.0 fusion.19
  117.3 0.0 all-gather.6.cloned.1.call-update
  117.3 0.0 all-reduce.6.cloned.1.call-start
  117.3 36.0 %all-gather.6.cloned.1.call-done = bf16[8192,256]{1,0:T(8,128)(2,1)} async-done(((bf16[1024,256]{1,0:T(8,128)(2,1)}), bf16[8192,256]{1,0:T(8,128)(2,1)}) %all-gather.6.cloned.1.call-update) | async-done | bytes 4194320 | tf_op jit(solution)/shard_map/all_gather | solution.py:16
  153.3 14.8 %fusion.15 = f32[1024,256]{1,0:T(8,128)} fusion(bf16[8192,256]{1,0:T(8,128)(2,1)} %all-gather.6.cloned.1.call-done, bf16[1,8192,1024]{2,1,0:T(8,128)(2,1)} %param.3, f32[1024,256]{1,0:T(8,128)S(1)} %copy-done, f32[1024,256]{1,0:T(8,128)S(1)} %copy-done.3, f32[256]{0:T(256)S(1)} %broadcast_multiply_fusion), kind=kOutput, calls=%fused_computation.9 | convolution fusion | flops 4297064448 | bytes 24118272 | tf_op jit(solution)/shard_map/dot_general | solution.py:14
  168.1 0.0 all-reduce.6.cloned.1.call-update
  168.1 0.2 all-gather.8.cloned.1.call-start
  168.4 51.8 %all-reduce.6.cloned.1.call-done = f32[1024,256]{1,0:T(8,128)} async-done(((f32[1024,256]{1,0:T(8,128)}), f32[1024,256]{1,0:T(8,128)}) %all-reduce.6.cloned.1.call-update) | async-done | bytes 1048592 | tf_op jit(solution)/shard_map/psum | solution.py:23
  220.2 2.9 fusion.21
  223.1 0.0 all-gather.8.cloned.1.call-update
  223.2 0.0 all-reduce.8.cloned.1.call-start
  223.2 36.0 %all-gather.8.cloned.1.call-done = bf16[8192,256]{1,0:T(8,128)(2,1)} async-done(((bf16[1024,256]{1,0:T(8,128)(2,1)}), bf16[8192,256]{1,0:T(8,128)(2,1)}) %all-gather.8.cloned.1.call-update) | async-done | bytes 4194320 | tf_op jit(solution)/shard_map/all_gather | solution.py:16
  259.2 14.8 %fusion.12 = f32[1024,256]{1,0:T(8,128)} fusion(bf16[8192,256]{1,0:T(8,128)(2,1)} %all-gather.8.cloned.1.call-done, bf16[1,8192,1024]{2,1,0:T(8,128)(2,1)} %param.3, f32[1024,256]{1,0:T(8,128)S(1)} %copy-done.2, f32[1024,256]{1,0:T(8,128)S(1)} %copy-done.4, f32[256]{0:T(256)S(1)} %broadcast_multiply_fusion), kind=kOutput, calls=%fused_computation.8 | convolution fusion | flops 4297064448 | bytes 24118272 | tf_op jit(solution)/shard_map/dot_general | solution.py:14
  274.0 52.1 %all-reduce.8.cloned.1.call-done = f32[1024,256]{1,0:T(8,128)} async-done(((f32[1024,256]{1,0:T(8,128)}), f32[1024,256]{1,0:T(8,128)}) %all-reduce.8.cloned.1.call-update) | async-done | bytes 1048592 | tf_op jit(solution)/shard_map/psum | solution.py:23
  326.1 3.3 subtract_bitcast_fusion
  (14 shorter events, 0.0 us)
Async XLA Ops:
  7.2 42.6 %all-gather.4.cloned.1.call-start = ((), (), s32[]{:S(2)}) async-start(), calls=%async_computation | async-start | bytes 4718592 | tf_op jit(solution)/shard_map/all_gather | solution.py:16
  9.3 53.0 %copy-start.5 = (f32[256]{0:T(256)S(1)}, f32[256]{0:T(256)}, u32[]{:S(2)}) copy-start(f32[256]{0:T(256)} %param.5) | copy-start | bytes 3076
  9.3 105.0 %copy-start.1 = (f32[1,1024,256]{2,1,0:T(8,128)S(1)}, f32[1,1024,256]{2,1,0:T(8,128)}, u32[]{:S(2)}) copy-start(f32[1,1024,256]{2,1,0:T(8,128)} %param.4) | copy-start | bytes 3145732
  9.3 105.0 %all-reduce.4.cloned.1.call-start = ((), (), s32[]{:S(2)}) async-start(), calls=%async_computation.1 | async-start | bytes 2097152 | tf_op jit(solution)/shard_map/psum | solution.py:23
  62.2 91.1 %copy-start = (f32[1024,256]{1,0:T(8,128)S(1)}, f32[1024,256]{1,0:T(8,128)}, u32[]{:S(2)}) copy-start(f32[1024,256]{1,0:T(8,128)} %fusion.4) | copy-start | bytes 3145732
  62.2 91.0 %all-gather.6.cloned.1.call-start = ((), (), s32[]{:S(2)}) async-start(), calls=%async_computation.2 | async-start | bytes 4718592 | tf_op jit(solution)/shard_map/all_gather | solution.py:16
  114.3 39.0 %copy-start.3 = (f32[1024,256]{1,0:T(8,128)S(1)}, f32[1024,256]{1,0:T(8,128)}, u32[]{:S(2)}) copy-start(f32[1024,256]{1,0:T(8,128)} %all-reduce.4.cloned.1.call-done) | copy-start | bytes 3145732
  117.3 102.9 %all-reduce.6.cloned.1.call-start = ((), (), s32[]{:S(2)}) async-start(), calls=%async_computation.3 | async-start | bytes 2097152 | tf_op jit(solution)/shard_map/psum | solution.py:23
  168.1 91.1 %copy-start.2 = (f32[1024,256]{1,0:T(8,128)S(1)}, f32[1024,256]{1,0:T(8,128)}, u32[]{:S(2)}) copy-start(f32[1024,256]{1,0:T(8,128)} %fusion.15) | copy-start | bytes 3145732
  168.1 91.0 %all-gather.8.cloned.1.call-start = ((), (), s32[]{:S(2)}) async-start(), calls=%async_computation.4 | async-start | bytes 4718592 | tf_op jit(solution)/shard_map/all_gather | solution.py:16
  220.2 39.0 %copy-start.4 = (f32[1024,256]{1,0:T(8,128)S(1)}, f32[1024,256]{1,0:T(8,128)}, u32[]{:S(2)}) copy-start(f32[1024,256]{1,0:T(8,128)} %all-reduce.6.cloned.1.call-done) | copy-start | bytes 3145732
  223.2 102.9 %all-reduce.8.cloned.1.call-start = ((), (), s32[]{:S(2)}) async-start(), calls=%async_computation.5 | async-start | bytes 2097152 | tf_op jit(solution)/shard_map/psum | solution.py:23
Sparse Core Ops, SparseCore 0:
  10.4 39.2 all-gather.3
  62.4 51.8 all-reduce.3
  117.4 35.8 all-gather.5
  168.2 51.8 all-reduce.5
  223.3 35.8 all-gather.7
  274.1 51.8 all-reduce.7
where the time goes:
time: 336 us
  waiting for transfers between devices  268 us (80%)
  matrix products  42.1 us (13%)
  between operations  14.1 us (4%)
  other arithmetic  11.3 us (3%)
    psum x3, waiting for transfers between devices, agree(): summed = lax.psum(summed_in, 'grp')  156 us
    all_gather x3, waiting for transfers between devices, apply_inverse(): lax.all_gather(shifted, 'col', axis=0, tiled=True)  112 us
    dot_general x3, matrix products, apply_inverse(): lax.dot_general(columns, lax.all_gather(shifted, 'col', axis=0, tiled=Tru...  42.1 us
    convert_element_type x3, other arithmetic, update_paths(): shifted = (right_part + consensus - duals).astype(jnp.bfloat16)  7.97 us
  transfers between devices with their start and end apart: 6, of which 6 were waited for; matrix products, arithmetic and copies ran while one was open for 0% of the time, Pallas kernels for 0%

commit v1 on v0

--- a/solution.py
+++ b/solution.py
@@ -20,7 +20,9 @@
 
 
 def agree(summed_in, limit, groups):
-    summed = lax.psum(summed_in, "grp")
+    summed = summed_in
+    for hop in (1, 2):
+        summed = summed + lax.ppermute(summed, "grp", [(dev, dev ^ hop) for dev in range(4)])
     return soft_shrink(summed / groups, limit[None, :])
 
 

time: 336 us -> 395 us (1.18)
  waiting for transfers between devices: 268 us -> 321 us
  starting transfers between devices: 0.43 us -> 12.4 us
  matrix products: 42.1 us -> 37.8 us
  other arithmetic: 11.3 us -> 7.17 us
    ppermute x0 -> x6, waiting for transfers between devices: none -> 208 us  [agree(): lax.ppermute(summed, 'grp', [(dev, dev ^ hop) for dev in range(4)])]
    psum x3 -> x0, waiting for transfers between devices: 156 us -> none  [agree(): summed = lax.psum(summed_in, 'grp')]
    ppermute x0 -> x6, starting transfers between devices: none -> 12.1 us  [agree(): lax.ppermute(summed, 'grp', [(dev, dev ^ hop) for dev in range(4)])]
    dot_general x3, matrix products: 42.1 us -> 37.8 us  [apply_inverse(): lax.dot_general(columns, lax.all_gather(shifted, 'col', axis=0, tiled=Tru...]
  transfers between devices with their start and end apart: 6 -> 9, of which waited for: 6 -> 9; matrix products, arithmetic and copies ran while one was open for 0% -> 0% of each run, Pallas kernels for 0% -> 0%
where the time goes in v1:
time: 395 us; the launch traced here: 394 us
  waiting for transfers between devices  321 us (81%)
  matrix products  37.8 us (10%)
  between operations  13.8 us (3%)
  starting transfers between devices  12.4 us (3%)
  other arithmetic  7.17 us (2%)
    ppermute x6, waiting for transfers between devices, agree(): lax.ppermute(summed, 'grp', [(dev, dev ^ hop) for dev in range(4)])  208 us
    all_gather x3, waiting for transfers between devices, apply_inverse(): lax.all_gather(shifted, 'col', axis=0, tiled=True)  114 us
    dot_general x3, matrix products, apply_inverse(): lax.dot_general(columns, lax.all_gather(shifted, 'col', axis=0, tiled=Tru...  37.8 us
    ppermute x6, starting transfers between devices, agree(): lax.ppermute(summed, 'grp', [(dev, dev ^ hop) for dev in range(4)])  12.1 us
  transfers between devices with their start and end apart: 9, of which 9 were waited for; matrix products, arithmetic and copies ran while one was open for 0% of the time, Pallas kernels for 0%

profile of v1, /device:TPU:0, one launch (start us, length us, event | category | flops | bytes accessed | tf_op | source)
XLA Modules:
  0.0 394.4 jit_solution(403176271780000812)
XLA Ops:
  7.2 2.1 bitcast_convert_fusion
  9.4 40.4 %all-gather.4.cloned.1.call-done = bf16[8192,256]{1,0:T(8,128)(2,1)} async-done(((bf16[1024,256]{1,0:T(8,128)(2,1)}), bf16[8192,256]{1,0:T(8,128)(2,1)}) %all-gather.4.cloned.1.call-update) | async-done | bytes 4194320 | tf_op jit(solution)/shard_map/all_gather | solution.py:16
  49.8 9.4 %fusion.4 = f32[1024,256]{1,0:T(8,128)S(1)} fusion(bf16[8192,256]{1,0:T(8,128)(2,1)} %all-gather.4.cloned.1.call-done, bf16[1,8192,1024]{2,1,0:T(8,128)(2,1)} %param.3), kind=kOutput, calls=%fused_computation.4 | convolution fusion | flops 4294967296 | bytes 22020096 | tf_op jit(solution)/shard_map/dot_general | solution.py:14
  59.2 1.5 collective-permute-start
  60.8 23.8 %collective-permute-done = f32[1024,256]{1,0:T(8,128)S(1)} collective-permute-done((f32[1024,256]{1,0:T(8,128)S(1)}, f32[1024,256]{1,0:T(8,128)S(1)}, u32[]{:S(2)}, u32[]{:S(2)}) %collective-permute-start) | collective-permute-done | bytes 1048608 | tf_op jit(solution)/shard_map/ppermute | solution.py:25
  84.7 2.5 collective-permute-start.1
  87.2 45.4 %collective-permute-done.1 = f32[1024,256]{1,0:T(8,128)S(1)} collective-permute-done((f32[1024,256]{1,0:T(8,128)S(1)}, f32[1024,256]{1,0:T(8,128)S(1)}, u32[]{:S(2)}, u32[]{:S(2)}) %collective-permute-start.1) | collective-permute-done | bytes 1048608 | tf_op jit(solution)/shard_map/ppermute | solution.py:25
  132.6 1.0 copy-done.2
  133.6 1.4 fusion.19
  135.3 36.5 %all-gather.6.cloned.1.call-done = bf16[8192,256]{1,0:T(8,128)(2,1)} async-done(((bf16[1024,256]{1,0:T(8,128)(2,1)}), bf16[8192,256]{1,0:T(8,128)(2,1)}) %all-gather.6.cloned.1.call-update) | async-done | bytes 4194320 | tf_op jit(solution)/shard_map/all_gather | solution.py:16
  171.8 14.3 %fusion.15 = f32[1024,256]{1,0:T(8,128)S(1)} fusion(bf16[8192,256]{1,0:T(8,128)(2,1)} %all-gather.6.cloned.1.call-done, bf16[1,8192,1024]{2,1,0:T(8,128)(2,1)} %param.3, f32[1024,256]{1,0:T(8,128)S(1)} %fusion.4, f32[256]{0:T(256)S(1)} %broadcast_multiply_fusion, f32[1024,256]{1,0:T(8,128)} %copy-done.1, f32[1024,256]{1,0:T(8,128)} %copy-done.2), kind=kOutput, calls=%fused_computation.9 | convolution fusion | flops 4297326592 | bytes 25166848 | tf_op jit(solution)/shard_map/dot_general | solution.py:14
  186.1 1.6 collective-permute-start.2
  187.6 23.8 %collective-permute-done.2 = f32[1024,256]{1,0:T(8,128)S(1)} collective-permute-done((f32[1024,256]{1,0:T(8,128)S(1)}, f32[1024,256]{1,0:T(8,128)S(1)}, u32[]{:S(2)}, u32[]{:S(2)}) %collective-permute-start.2) | collective-permute-done | bytes 1048608 | tf_op jit(solution)/shard_map/ppermute | solution.py:25
  211.6 2.5 collective-permute-start.3
  214.1 45.4 %collective-permute-done.3 = f32[1024,256]{1,0:T(8,128)S(1)} collective-permute-done((f32[1024,256]{1,0:T(8,128)S(1)}, f32[1024,256]{1,0:T(8,128)S(1)}, u32[]{:S(2)}, u32[]{:S(2)}) %collective-permute-start.3) | collective-permute-done | bytes 1048608 | tf_op jit(solution)/shard_map/ppermute | solution.py:25
  259.5 1.0 copy-done.3
  260.5 1.4 fusion.21
  261.9 36.7 %all-gather.8.cloned.1.call-done = bf16[8192,256]{1,0:T(8,128)(2,1)} async-done(((bf16[1024,256]{1,0:T(8,128)(2,1)}), bf16[8192,256]{1,0:T(8,128)(2,1)}) %all-gather.8.cloned.1.call-update) | async-done | bytes 4194320 | tf_op jit(solution)/shard_map/all_gather | solution.py:16
  298.6 14.0 %fusion.12 = f32[1024,256]{1,0:T(8,128)S(1)} fusion(bf16[8192,256]{1,0:T(8,128)(2,1)} %all-gather.8.cloned.1.call-done, bf16[1,8192,1024]{2,1,0:T(8,128)(2,1)} %param.3, f32[1024,256]{1,0:T(8,128)S(1)} %fusion.15, f32[256]{0:T(256)S(1)} %broadcast_multiply_fusion, f32[1024,256]{1,0:T(8,128)S(1)} %add.36, f32[1024,256]{1,0:T(8,128)} %copy-done.3), kind=kOutput, calls=%fused_computation.8 | convolution fusion | flops 4297326592 | bytes 25166848 | tf_op jit(solution)/shard_map/dot_general | solution.py:14
  312.7 1.6 collective-permute-start.4
  314.2 23.8 %collective-permute-done.4 = f32[1024,256]{1,0:T(8,128)S(1)} collective-permute-done((f32[1024,256]{1,0:T(8,128)S(1)}, f32[1024,256]{1,0:T(8,128)S(1)}, u32[]{:S(2)}, u32[]{:S(2)}) %collective-permute-start.4) | collective-permute-done | bytes 1048608 | tf_op jit(solution)/shard_map/ppermute | solution.py:25
  338.2 2.5 collective-permute-start.5
  340.6 45.4 %collective-permute-done.5 = f32[1024,256]{1,0:T(8,128)S(1)} collective-permute-done((f32[1024,256]{1,0:T(8,128)S(1)}, f32[1024,256]{1,0:T(8,128)S(1)}, u32[]{:S(2)}, u32[]{:S(2)}) %collective-permute-start.5) | collective-permute-done | bytes 1048608 | tf_op jit(solution)/shard_map/ppermute | solution.py:25
  386.1 1.9 subtract_bitcast_fusion
  (18 shorter events, 0.8 us)
Async XLA Ops:
  7.2 42.6 %all-gather.4.cloned.1.call-start = ((), (), s32[]{:S(2)}) async-start(), calls=%async_computation | async-start | bytes 4718592 | tf_op jit(solution)/shard_map/all_gather | solution.py:16
  9.3 77.9 %copy-start.4 = (f32[256]{0:T(256)S(1)}, f32[256]{0:T(256)}, u32[]{:S(2)}) copy-start(f32[256]{0:T(256)} %param.5) | copy-start | bytes 3076
  9.3 124.3 %copy-start = (f32[1,1024,256]{2,1,0:T(8,128)S(1)}, f32[1,1024,256]{2,1,0:T(8,128)}, u32[]{:S(2)}) copy-start(f32[1,1024,256]{2,1,0:T(8,128)} %param.4) | copy-start | bytes 3145732
  9.3 162.4 %all-gather.6.cloned.1.call-start = ((), (), s32[]{:S(2)}) async-start(), calls=%async_computation.1 | async-start | bytes 4718592 | tf_op jit(solution)/shard_map/all_gather | solution.py:16
  59.2 25.4 %collective-permute-start = (f32[1024,256]{1,0:T(8,128)S(1)}, f32[1024,256]{1,0:T(8,128)S(1)}, u32[]{:S(2)}, u32[]{:S(2)}) collective-permute-start(f32[1024,256]{1,0:T(8,128)S(1)} %fusion.4), channel_id=1, source_target_pairs={{0,8},{8,0},{16,24},{24,16},{1,9},{9,1},{17,25},{25,17},{2,10},{10... | collective-permute-start | bytes 3145736 | tf_op jit(solution)/shard_map/ppermute | solution.py:25
  84.7 47.9 %copy-start.1 = (f32[1024,256]{1,0:T(8,128)}, f32[1024,256]{1,0:T(8,128)S(1)}, u32[]{:S(2)}) copy-start(f32[1024,256]{1,0:T(8,128)S(1)} %add.32) | copy-start | bytes 3145732
  84.7 47.9 %collective-permute-start.1 = (f32[1024,256]{1,0:T(8,128)S(1)}, f32[1024,256]{1,0:T(8,128)S(1)}, u32[]{:S(2)}, u32[]{:S(2)}) collective-permute-start(f32[1024,256]{1,0:T(8,128)S(1)} %add.32), channel_id=1, source_target_pairs={{0,16},{8,24},{16,0},{24,8},{1,17},{9,25},{17,1},{25,9},{2,18},{10... | collective-permute-start | bytes 3145736 | tf_op jit(solution)/shard_map/ppermute | solution.py:25
  132.6 1.0 copy-start.2
  135.1 163.6 %all-gather.8.cloned.1.call-start = ((), (), s32[]{:S(2)}) async-start(), calls=%async_computation.2 | async-start | bytes 4718592 | tf_op jit(solution)/shard_map/all_gather | solution.py:16
  186.1 25.4 %collective-permute-start.2 = (f32[1024,256]{1,0:T(8,128)S(1)}, f32[1024,256]{1,0:T(8,128)S(1)}, u32[]{:S(2)}, u32[]{:S(2)}) collective-permute-start(f32[1024,256]{1,0:T(8,128)S(1)} %fusion.15), channel_id=1, source_target_pairs={{0,8},{8,0},{16,24},{24,16},{1,9},{9,1},{17,25},{25,17},{2,10},{10... | collective-permute-start | bytes 3145736 | tf_op jit(solution)/shard_map/ppermute | solution.py:25
  211.6 47.9 %collective-permute-start.3 = (f32[1024,256]{1,0:T(8,128)S(1)}, f32[1024,256]{1,0:T(8,128)S(1)}, u32[]{:S(2)}, u32[]{:S(2)}) collective-permute-start(f32[1024,256]{1,0:T(8,128)S(1)} %add.36), channel_id=1, source_target_pairs={{0,16},{8,24},{16,0},{24,8},{1,17},{9,25},{17,1},{25,9},{2,18},{10... | collective-permute-start | bytes 3145736 | tf_op jit(solution)/shard_map/ppermute | solution.py:25
  259.5 1.0 copy-start.3
  312.7 25.4 %collective-permute-start.4 = (f32[1024,256]{1,0:T(8,128)S(1)}, f32[1024,256]{1,0:T(8,128)S(1)}, u32[]{:S(2)}, u32[]{:S(2)}) collective-permute-start(f32[1024,256]{1,0:T(8,128)S(1)} %fusion.12), channel_id=1, source_target_pairs={{0,8},{8,0},{16,24},{24,16},{1,9},{9,1},{17,25},{25,17},{2,10},{10... | collective-permute-start | bytes 3145736 | tf_op jit(solution)/shard_map/ppermute | solution.py:25
  338.2 47.9 %collective-permute-start.5 = (f32[1024,256]{1,0:T(8,128)S(1)}, f32[1024,256]{1,0:T(8,128)S(1)}, u32[]{:S(2)}, u32[]{:S(2)}) collective-permute-start(f32[1024,256]{1,0:T(8,128)S(1)} %add.40), channel_id=1, source_target_pairs={{0,16},{8,24},{16,0},{24,8},{1,17},{9,25},{17,1},{25,9},{2,18},{10... | collective-permute-start | bytes 3145736 | tf_op jit(solution)/shard_map/ppermute | solution.py:25
Sparse Core Ops, SparseCore 0:
  10.4 39.2 all-gather.3
  135.2 36.5 all-gather.5
  262.0 36.5 all-gather.7
